TPU v7x, 32 devices: a whole 2x2x4 slice. The times are simulated.
32 devices in a mesh: ri: 8 (over z, core), rj: 4 (over y, x).
Axes of the slice: x: 2, y: 2, z: 4, core: 2. Of those that a mesh axis runs over, the one named last changes fastest.
Arguments:
- pair: bfloat16 [320, 320, 128], P('ri', 'rj'), may hold values from -6 to 6
- in_gain: float32 [128], replicated, may hold values from 0.1 to 1.9
- in_bias: float32 [128], replicated, may hold values from -3 to 3
- w_in: bfloat16 [128, 512], replicated, may hold values from -0.5 to 0.5
- w_gate: bfloat16 [128, 128], replicated, may hold values from -0.5 to 0.5
- out_gain: float32 [128], replicated, may hold values from 0.1 to 1.9
- out_bias: float32 [128], replicated, may hold values from -3 to 3
- w_out: bfloat16 [128, 128], replicated, may hold values from -0.5 to 0.5
Outputs:
- update: bfloat16 [320, 320, 128], P('ri', 'rj')
All inputs are finite; a program needn't handle non-finite values.
Results may differ from a plain program's by a relative error of at most 0.015.
Values may be sent and summed in bfloat16 or wider, within the bound.
A program may use at most 128 MiB of HBM per device.

v0:
```python
import jax
import jax.numpy as jnp
from jax import lax
from jax.sharding import PartitionSpec as P


def layer_norm(values, gain, bias):
    mean = jnp.mean(values, axis=-1, keepdims=True)
    centered = values - mean
    var = jnp.mean(centered * centered, axis=-1, keepdims=True)
    return centered * lax.rsqrt(var + 1e-05) * gain + bias


def local(pair, in_gain, in_bias, w_in, w_gate, out_gain, out_bias, w_out):
    rows, cols, chans = pair.shape
    hidden = w_out.shape[0]
    normed = layer_norm(pair.astype(jnp.float32), in_gain, in_bias).astype(jnp.bfloat16)
    flat = normed.reshape(rows * cols, chans)
    proj = jnp.dot(flat, w_in, preferred_element_type=jnp.float32)
    a_tile = (
        (jax.nn.sigmoid(proj[:, hidden : 2 * hidden]) * proj[:, :hidden])
        .astype(jnp.bfloat16)
        .reshape(rows, cols, hidden)
    )
    b_tile = (
        (jax.nn.sigmoid(proj[:, 3 * hidden :]) * proj[:, 2 * hidden : 3 * hidden])
        .astype(jnp.bfloat16)
        .reshape(rows, cols, hidden)
    )
    gate = jax.nn.sigmoid(jnp.dot(flat, w_gate, preferred_element_type=jnp.float32)).astype(
        jnp.bfloat16
    )
    a_rows = lax.all_gather(a_tile, "rj", axis=1, tiled=True)
    product = lax.dot_general(
        a_rows, b_tile, (((0,), (0,)), ((2,), (2,))), preferred_element_type=jnp.float32
    )
    summed = lax.psum_scatter(
        jnp.transpose(product, (1, 2, 0)).astype(jnp.bfloat16),
        "ri",
        scatter_dimension=0,
        tiled=True,
    ).astype(jnp.float32)
    tri = summed.reshape(rows * cols, hidden)
    tri_normed = layer_norm(tri, out_gain, out_bias).astype(jnp.bfloat16)
    mixed = jnp.dot(tri_normed, w_out, preferred_element_type=jnp.float32)
    update = gate.astype(jnp.float32) * mixed
    return update.reshape(rows, cols, chans).astype(jnp.bfloat16)


def solution(mesh):
    return jax.shard_map(
        local,
        mesh=mesh,
        in_specs=(P("ri", "rj", None), P(), P(), P(), P(), P(), P(), P()),
        out_specs=P("ri", "rj", None),
        check_vma=False,
    )
```

profile of v0, /device:TPU:0, one launch (start us, length us, event | category | flops | bytes accessed | tf_op | source)
XLA Modules:
  0.0 174.6 jit_solution(12855295967835624654)
XLA Ops:
  6.5 0.0 copy-start
  6.5 0.0 copy-start.1
  6.5 0.0 copy-start.4
  6.5 0.0 copy-start.5
  6.5 0.0 all-gather.2.cloned.1.call-start
  6.6 1.6 convert_reduce_fusion
  8.2 2.3 %fusion.8 = f32[40,80]{1,0:T(8,128)S(1)} fusion(bf16[40,80,128]{2,1,0:T(8,128)(2,1)} %param.8, f32[40,80]{1,0:T(8,128)S(1)} %broadcast_multiply_fusion.1), kind=kLoop, calls=%fused_computation.13 | loop fusion | flops 1635200 | bytes 844800 | tf_op jit(solution)/shard_map/reduce_sum | solution.py:10
  10.6 0.0 copy-done.1
  10.6 0.0 copy-done.4
  10.6 0.0 copy-done.5
  10.6 1.1 fusion.11
  11.7 0.0 copy-done
  11.7 1.0 fusion.24
  12.7 0.9 fusion.12
  13.6 1.1 copy.28
  14.7 0.0 all-gather.2.cloned.1.call-update
  14.7 0.0 reduce-scatter.2.cloned.1.call-start
  14.8 1.6 copy.30
  16.4 46.1 %all-gather.2.cloned.1.call-done = bf16[40,320,128]{2,0,1:T(8,128)(2,1)} async-done(((bf16[40,80,128]{2,0,1:T(8,128)(2,1)}), bf16[40,320,128]{2,0,1:T(8,128)(2,1)}) %all-gather.2.cloned.1.call-update) | async-done | bytes 3276816 | tf_op jit(solution)/shard_map/all_gather | solution.py:33
  62.5 6.7 %copy.29 = bf16[40,320,128]{1,0,2:T(8,128)(2,1)} copy(bf16[40,320,128]{2,0,1:T(8,128)(2,1)} %all-gather.2.cloned.1.call-done) | data formatting | bytes 6553600 | tf_op jit(solution)/shard_map/all_gather | solution.py:33
  69.3 7.4 %convert_bitcast_fusion = bf16[320,80,128]{0,1,2:T(8,128)(2,1)} fusion(bf16[40,320,128]{1,0,2:T(8,128)(2,1)} %copy.29, bf16[40,80,128]{1,0,2:T(8,128)(2,1)S(1)} %copy.30), kind=kOutput, calls=%fused_computation | convolution fusion | flops 265420800 | bytes 10649600 | tf_op jit(solution)/shard_map/dot_general | solution.py:34
  76.7 11.5 %copy.31 = bf16[320,80,128]{2,1,0:T(8,128)(2,1)} copy(bf16[320,80,128]{0,1,2:T(8,128)(2,1)} %convert_bitcast_fusion) | data formatting | bytes 13107200 | tf_op jit(solution)/shard_map/convert_element_type | solution.py:38
  88.2 0.0 copy-start.8
  88.2 0.0 reduce-scatter.2.cloned.1.call-update
  88.2 0.7 copy-done.8
  89.0 0.6 fusion.4
  89.5 0.0 copy-start.6
  89.6 0.0 copy-start.7
  89.6 0.0 copy-start.3
  89.6 71.0 %reduce-scatter.2.cloned.1.call-done = bf16[40,80,128]{2,1,0:T(8,128)(2,1)} async-done(((bf16[320,80,128]{2,1,0:T(8,128)(2,1)}), bf16[40,80,128]{2,1,0:T(8,128)(2,1)}) %reduce-scatter.2.cloned.1.call-update) | async-done | bytes 819216 | tf_op jit(solution)/shard_map/reduce_scatter | solution.py:37
  160.6 0.0 copy-start.2
  160.6 1.6 convert_reduce_fusion.1
  162.2 0.1 div.29
  162.3 2.3 %multiply_reduce_fusion = f32[40,80]{1,0:T(8,128)S(1)} fusion(f32[40,80]{1,0:T(8,128)S(1)} %broadcast_multiply_fusion, bf16[40,80,128]{2,1,0:T(8,128)(2,1)} %reduce-scatter.2.cloned.1.call-done), kind=kLoop, calls=%fused_computation.34 | loop fusion | flops 1635200 | bytes 844800 | tf_op jit(solution)/shard_map/reduce_sum | solution.py:10
  164.7 0.1 rsqrt.21
  164.8 0.0 copy-done.6
  164.8 0.0 copy-done.7
  164.8 0.0 copy-done.2
  164.8 1.7 %fusion.23 = bf16[3200,128]{1,0:T(8,128)(2,1)S(1)} fusion(f32[128]{0:T(128)S(1)} %copy-done.6, f32[128]{0:T(128)S(1)} %copy-done.7, f32[3200]{0:T(1024)S(1)} %rsqrt.21, f32[3200]{0:T(1024)S(1)} %div.29, bf16[40,80,128]{2,1,0:T(8,128)(2,1)S(1)} %copy-done.2), kind=kLoop, calls=%fused_computation.33 | loop fusion | flops 2457600 | bytes 1665024 | tf_op jit(solution)/shard_map/convert_element_type | solution.py:44
  166.5 0.0 copy-done.3
  166.5 1.2 fusion.5
  (4 shorter events, 0.0 us)
Async XLA Ops:
  6.5 5.2 %copy-start = (bf16[128,512]{1,0:T(8,128)(2,1)S(1)}, bf16[128,512]{1,0:T(8,128)(2,1)}, u32[]{:S(2)}) copy-start(bf16[128,512]{1,0:T(8,128)(2,1)} %param.11) | copy-start | bytes 393220
  6.5 4.1 %copy-start.1 = (bf16[40,80,128]{2,1,0:T(8,128)(2,1)S(1)}, bf16[40,80,128]{2,1,0:T(8,128)(2,1)}, u32[]{:S(2)}) copy-start(bf16[40,80,128]{2,1,0:T(8,128)(2,1)} %param.8) | copy-start | bytes 2457604
  6.5 4.1 %copy-start.4 = (f32[128]{0:T(128)S(1)}, f32[128]{0:T(128)}, u32[]{:S(2)}) copy-start(f32[128]{0:T(128)} %param.10) | copy-start | bytes 1540
  6.5 4.1 %copy-start.5 = (f32[128]{0:T(128)S(1)}, f32[128]{0:T(128)}, u32[]{:S(2)}) copy-start(f32[128]{0:T(128)} %param.9) | copy-start | bytes 1540
  6.5 56.0 %all-gather.2.cloned.1.call-start = ((), (), s32[]{:S(2)}) async-start(), calls=%async_computation.1 | async-start | bytes 4096000 | tf_op jit(solution)/shard_map/all_gather | solution.py:33
  14.7 145.9 %reduce-scatter.2.cloned.1.call-start = ((), (), s32[]{:S(2)}) async-start(), calls=%async_computation.2 | async-start | bytes 7372800 | tf_op jit(solution)/shard_map/reduce_scatter | solution.py:37
  88.2 0.8 copy-start.8
  89.5 75.2 %copy-start.6 = (f32[128]{0:T(128)S(1)}, f32[128]{0:T(128)}, u32[]{:S(2)}) copy-start(f32[128]{0:T(128)} %param.14) | copy-start | bytes 1540
  89.6 75.2 %copy-start.7 = (f32[128]{0:T(128)S(1)}, f32[128]{0:T(128)}, u32[]{:S(2)}) copy-start(f32[128]{0:T(128)} %param.13) | copy-start | bytes 1540
  89.6 77.0 %copy-start.3 = (bf16[128,128]{1,0:T(8,128)(2,1)S(1)}, bf16[128,128]{1,0:T(8,128)(2,1)}, u32[]{:S(2)}) copy-start(bf16[128,128]{1,0:T(8,128)(2,1)} %param.15) | copy-start | bytes 98308
  160.6 4.2 %copy-start.2 = (bf16[40,80,128]{2,1,0:T(8,128)(2,1)S(1)}, bf16[40,80,128]{2,1,0:T(8,128)(2,1)}, u32[]{:S(2)}) copy-start(bf16[40,80,128]{2,1,0:T(8,128)(2,1)} %reduce-scatter.2.cloned.1.call-done) | copy-start | bytes 2457604
Sparse Core Ops, SparseCore 0:
  14.8 47.6 all-gather.1
  88.4 72.1 reduce-scatter.1
where the time goes:
time: 175 us
  waiting for transfers between devices  117 us (67%)
  local copies, waits for them, and re-layouts  21.9 us (13%)
  between operations  13.6 us (8%)
  other arithmetic  11.7 us (7%)
  matrix products  10.2 us (6%)
    reduce_scatter x1, waiting for transfers between devices, local(): lax.psum_scatter(jnp.transpose(product, (1, 2, 0)).astype(jnp.bfloat16),...  71 us
    all_gather x1, waiting for transfers between devices, local(): a_rows = lax.all_gather(a_tile, 'rj', axis=1, tiled=True)  46.1 us
    convert_element_type x1, local copies, waits for them, and re-layouts, local(): jnp.transpose(product, (1, 2, 0)).astype(jnp.bfloat16)  11.5 us
    dot_general x1, matrix products, local(): lax.dot_general(a_rows, b_tile, (((0,), (0,)), ((2,), (2,))), preferred_e...  7.43 us
    all_gather x1, local copies, waits for them, and re-layouts, local(): a_rows = lax.all_gather(a_tile, 'rj', axis=1, tiled=True)  6.75 us
    reduce_sum x2, other arithmetic, layer_norm(): var = jnp.mean(centered * centered, axis=-1, keepdims=True)  4.67 us
  transfers between devices with their start and end apart: 2, of which 2 were waited for; matrix products, arithmetic and copies ran while one was open for 1% of the time, Pallas kernels for 0%

commit v1 on v0

--- a/solution.py
+++ b/solution.py
@@ -30,7 +30,15 @@
     gate = jax.nn.sigmoid(jnp.dot(flat, w_gate, preferred_element_type=jnp.float32)).astype(
         jnp.bfloat16
     )
-    a_rows = lax.all_gather(a_tile, "rj", axis=1, tiled=True)
+    axis_len = jax.lax.axis_size("rj")
+    k_now = [None] * axis_len
+    k_now[axis_len - 1] = a_tile
+    shelf = [(pp, (pp + 1) % axis_len) for pp in range(axis_len)]
+    for jj in range(axis_len - 2, -1, -1):
+        k_now[jj] = jax.lax.ppermute(k_now[jj + 1], axis_name="rj", perm=shelf)
+    h_now = jnp.concatenate(k_now, axis=1)
+    piece_now = (jax.lax.axis_index("rj") + 1) * a_tile.shape[1]
+    a_rows = jnp.roll(h_now, piece_now, axis=1)
     product = lax.dot_general(
         a_rows, b_tile, (((0,), (0,)), ((2,), (2,))), preferred_element_type=jnp.float32
     )

time: 175 us -> 202 us (1.15)
  local copies, waits for them, and re-layouts: 21.9 us -> 39.7 us
  waiting for transfers between devices: 117 us -> 121 us
  starting transfers between devices: 0.08 us -> 3.84 us
    ppermute x0 -> x3, waiting for transfers between devices: none -> 50.1 us  [local(): k_now[jj] = jax.lax.ppermute(k_now[jj + 1], axis_name='rj', perm=shelf)]
    all_gather x1 -> x0, waiting for transfers between devices: 46.1 us -> none  [local(): a_rows = lax.all_gather(a_tile, 'rj', axis=1, tiled=True)]
    concatenate x0 -> x1, local copies, waits for them, and re-layouts: none -> 14 us  [local(): a_rows = jnp.roll(h_now, piece_now, axis=1)]
    ppermute x0 -> x3, local copies, waits for them, and re-layouts: none -> 7.31 us  [local(): k_now[jj] = jax.lax.ppermute(k_now[jj + 1], axis_name='rj', perm=shelf)]
    all_gather x1 -> x0, local copies, waits for them, and re-layouts: 6.75 us -> none  [local(): a_rows = lax.all_gather(a_tile, 'rj', axis=1, tiled=True)]
    ppermute x0 -> x3, starting transfers between devices: none -> 3.81 us  [local(): k_now[jj] = jax.lax.ppermute(k_now[jj + 1], axis_name='rj', perm=shelf)]
    unnamed x18 -> x24, local copies, waits for them, and re-layouts: 0.77 us -> 2.95 us
  transfers between devices with their start and end apart: 2 -> 4, of which waited for: 2 -> 4; matrix products, arithmetic and copies ran while one was open for 1% -> 5% of each run, Pallas kernels for 0% -> 0%
where the time goes in v1:
time: 202 us; the launch traced here: 201 us
  waiting for transfers between devices  121 us (60%)
  local copies, waits for them, and re-layouts  39.7 us (20%)
  between operations  13.6 us (7%)
  other arithmetic  11.7 us (6%)
  matrix products  11.3 us (6%)
  starting transfers between devices  3.84 us (2%)
    reduce_scatter x1, waiting for transfers between devices, local(): lax.psum_scatter(jnp.transpose(product, (1, 2, 0)).astype(jnp.bfloat16),...  70.6 us
    ppermute x3, waiting for transfers between devices, local(): k_now[jj] = jax.lax.ppermute(k_now[jj + 1], axis_name='rj', perm=shelf)  50.1 us
    concatenate x1, local copies, waits for them, and re-layouts, local(): a_rows = jnp.roll(h_now, piece_now, axis=1)  14 us
    convert_element_type x1, local copies, waits for them, and re-layouts, local(): jnp.transpose(product, (1, 2, 0)).astype(jnp.bfloat16)  11.5 us
    dot_general x1, matrix products, local(): lax.dot_general(a_rows, b_tile, (((0,), (0,)), ((2,), (2,))), preferred_e...  8.47 us
    ppermute x3, local copies, waits for them, and re-layouts, local(): k_now[jj] = jax.lax.ppermute(k_now[jj + 1], axis_name='rj', perm=shelf)  7.31 us
    reduce_sum x2, other arithmetic, layer_norm(): var = jnp.mean(centered * centered, axis=-1, keepdims=True)  4.67 us
  transfers between devices with their start and end apart: 4, of which 4 were waited for; matrix products, arithmetic and copies ran while one was open for 5% of the time, Pallas kernels for 0%

profile of v1, /device:TPU:0, one launch (start us, length us, event | category | flops | bytes accessed | tf_op | source)
XLA Modules:
  0.0 200.8 jit_solution(8546305763321801935)
XLA Ops:
  6.5 0.0 copy-start
  6.5 0.0 copy-start.1
  6.5 0.0 copy-start.7
  6.5 0.0 reduce-scatter.2.cloned.1.call-start
  6.6 1.6 convert_reduce_fusion
  8.2 2.3 %fusion.9 = f32[40,80]{1,0:T(8,128)S(1)} fusion(bf16[40,80,128]{2,1,0:T(8,128)(2,1)} %param.8, f32[40,80]{1,0:T(8,128)S(1)} %broadcast_multiply_fusion.1), kind=kLoop, calls=%fused_computation.14 | loop fusion | flops 1635200 | bytes 844800 | tf_op jit(solution)/shard_map/reduce_sum | solution.py:10
  10.6 0.0 copy-done.1
  10.6 0.0 copy-done.7
  10.6 0.0 copy-done.8
  10.6 1.1 fusion.12
  11.7 0.0 copy-start.3
  11.7 0.9 copy-done.3
  12.6 0.0 copy-done
  12.6 1.0 fusion.26
  13.6 0.9 fusion.17
  14.5 3.0 %collective-permute-start = (bf16[40,80,128]{2,1,0:T(8,128)(2,1)S(1)}, bf16[40,80,128]{2,1,0:T(8,128)(2,1)S(1)}, u32[]{:S(2)}, u32[]{:S(2)}) collective-permute-start(bf16[40,80,128]{2,1,0:T(8,128)(2,1)S(1)} %bitcast.26), channel_id=1, source_target_pairs={{0,1},{1,2},{2,3},{3,0},{4,5},{5,6},{6,7},{7,4},{8,9},{9,10},{10,1... | collective-permute-start | bytes 2457608 | tf_op jit(solution)/shard_map/ppermute | solution.py:38
  17.5 19.2 %collective-permute-done = bf16[40,80,128]{2,1,0:T(8,128)(2,1)S(1)} collective-permute-done((bf16[40,80,128]{2,1,0:T(8,128)(2,1)S(1)}, bf16[40,80,128]{2,1,0:T(8,128)(2,1)S(1)}, u32[]{:S(2)}, u32[]{:S(2)}) %collective-permute-start) | collective-permute-done | bytes 819232 | tf_op jit(solution)/shard_map/ppermute | solution.py:38
  36.7 0.9 copy-done.5
  37.6 0.8 collective-permute-start.1
  38.4 19.6 %collective-permute-done.1 = bf16[40,80,128]{2,1,0:T(8,128)(2,1)} collective-permute-done((bf16[40,80,128]{2,1,0:T(8,128)(2,1)S(1)}, bf16[40,80,128]{2,1,0:T(8,128)(2,1)}, u32[]{:S(2)}, u32[]{:S(2)}) %collective-permute-start.1) | collective-permute-done | bytes 819232 | tf_op jit(solution)/shard_map/ppermute | solution.py:38
  58.0 0.0 collective-permute-start.2
  58.0 1.6 copy.41
  59.6 2.2 %copy.46 = bf16[40,80,128]{1,0,2:T(8,128)(2,1)} copy(bf16[40,80,128]{2,1,0:T(8,128)(2,1)S(1)} %bitcast.25) | data formatting | bytes 1638400 | tf_op jit(solution)/shard_map/reshape | solution.py:28
  61.8 2.0 %copy.40 = bf16[40,80,128]{1,0,2:T(8,128)(2,1)S(1)} copy(bf16[40,80,128]{2,1,0:T(8,128)(2,1)} %copy-done.5) | data formatting | bytes 1638400 | tf_op jit(solution)/shard_map/ppermute | solution.py:38
  63.8 2.7 %copy.39 = bf16[40,80,128]{1,0,2:T(8,128)(2,1)} copy(bf16[40,80,128]{2,1,0:T(8,128)(2,1)} %collective-permute-done.1) | data formatting | bytes 1638400 | tf_op jit(solution)/shard_map/ppermute | solution.py:38
  66.5 11.3 %collective-permute-done.2 = bf16[40,80,128]{2,1,0:T(8,128)(2,1)} collective-permute-done((bf16[40,80,128]{2,1,0:T(8,128)(2,1)}, bf16[40,80,128]{2,1,0:T(8,128)(2,1)}, u32[]{:S(2)}, u32[]{:S(2)}) %collective-permute-start.2) | collective-permute-done | bytes 819232 | tf_op jit(solution)/shard_map/ppermute | solution.py:38
  77.8 2.6 %copy.38 = bf16[40,80,128]{1,0,2:T(8,128)(2,1)} copy(bf16[40,80,128]{2,1,0:T(8,128)(2,1)} %collective-permute-done.2) | data formatting | bytes 1638400 | tf_op jit(solution)/shard_map/ppermute | solution.py:38
  80.4 14.0 %concatenate.6 = bf16[40,640,128]{1,0,2:T(8,128)(2,1)} concatenate(bf16[40,80,128]{1,0,2:T(8,128)(2,1)} %copy.38, bf16[40,80,128]{1,0,2:T(8,128)(2,1)} %copy.39, bf16[40,80,128]{1,0,2:T(8,128)(2,1)S(1)} %copy.40, bf16[40,80,128]{1,0,2:T(8,128)(2,1)S(1)} %copy.41, bf16[40,80,128]{1,0,2:T(8,128)(2,1)} %copy.38, bf16[40,80,128]{1,0,2:T(8,128)(2,1)} %copy.39, ...), dimensions={1} | concatenate | bytes 13107200 | tf_op jit(solution)/shard_map/jit(_roll_dynamic)/concatenate | solution.py:41
  94.4 8.5 %convert_bitcast_fusion = bf16[320,80,128]{0,1,2:T(8,128)(2,1)} fusion(bf16[40,80,128]{1,0,2:T(8,128)(2,1)} %copy.46, bf16[40,640,128]{1,0,2:T(8,128)(2,1)} %concatenate.6, s32[]{:T(128)S(6)} %select_n.14), kind=kOutput, calls=%fused_computation | convolution fusion | flops 265420800 | bytes 11796484 | tf_op jit(solution)/shard_map/dot_general | solution.py:42
  102.9 11.5 %copy.47 = bf16[320,80,128]{2,1,0:T(8,128)(2,1)} copy(bf16[320,80,128]{0,1,2:T(8,128)(2,1)} %convert_bitcast_fusion) | data formatting | bytes 13107200 | tf_op jit(solution)/shard_map/convert_element_type | solution.py:46
  114.4 0.0 reduce-scatter.2.cloned.1.call-update
  114.4 1.1 copy-done.4
  115.5 0.0 copy-done.11
  115.5 0.6 fusion.4
  116.1 0.0 copy-start.9
  116.1 0.0 copy-start.10
  116.1 0.0 copy-start.6
  116.2 70.6 %reduce-scatter.2.cloned.1.call-done = bf16[40,80,128]{2,1,0:T(8,128)(2,1)} async-done(((bf16[320,80,128]{2,1,0:T(8,128)(2,1)}), bf16[40,80,128]{2,1,0:T(8,128)(2,1)}) %reduce-scatter.2.cloned.1.call-update) | async-done | bytes 819216 | tf_op jit(solution)/shard_map/reduce_scatter | solution.py:45
  186.7 1.6 convert_reduce_fusion.1
  188.4 0.1 div.29
  188.5 2.3 %multiply_reduce_fusion = f32[40,80]{1,0:T(8,128)S(1)} fusion(f32[40,80]{1,0:T(8,128)S(1)} %broadcast_multiply_fusion, bf16[40,80,128]{2,1,0:T(8,128)(2,1)} %reduce-scatter.2.cloned.1.call-done), kind=kLoop, calls=%fused_computation.35 | loop fusion | flops 1635200 | bytes 844800 | tf_op jit(solution)/shard_map/reduce_sum | solution.py:10
  190.8 0.1 rsqrt.21
  190.9 0.0 copy-done.9
  190.9 0.0 copy-done.10
  190.9 0.0 copy-done.2
  190.9 1.7 fusion.24
  192.7 0.0 copy-done.6
  192.7 1.2 fusion.5
  (9 shorter events, 0.0 us)
Async XLA Ops:
  6.5 6.1 %copy-start = (bf16[128,512]{1,0:T(8,128)(2,1)S(1)}, bf16[128,512]{1,0:T(8,128)(2,1)}, u32[]{:S(2)}) copy-start(bf16[128,512]{1,0:T(8,128)(2,1)} %param.11) | copy-start | bytes 393220
  6.5 4.1 %copy-start.1 = (bf16[40,80,128]{2,1,0:T(8,128)(2,1)S(1)}, bf16[40,80,128]{2,1,0:T(8,128)(2,1)}, u32[]{:S(2)}) copy-start(bf16[40,80,128]{2,1,0:T(8,128)(2,1)} %param.8) | copy-start | bytes 2457604
  6.5 4.1 %copy-start.7 = (f32[128]{0:T(128)S(1)}, f32[128]{0:T(128)}, u32[]{:S(2)}) copy-start(f32[128]{0:T(128)} %param.10) | copy-start | bytes 1540
  6.5 4.1 %copy-start.8 = (f32[128]{0:T(128)S(1)}, f32[128]{0:T(128)}, u32[]{:S(2)}) copy-start(f32[128]{0:T(128)} %param.9) | copy-start | bytes 1540
  6.5 180.2 %reduce-scatter.2.cloned.1.call-start = ((), (), s32[]{:S(2)}) async-start(), calls=%async_computation.1 | async-start | bytes 7372800 | tf_op jit(solution)/shard_map/reduce_scatter | solution.py:45
  11.7 0.9 copy-start.3
  14.5 22.2 %collective-permute-start = (bf16[40,80,128]{2,1,0:T(8,128)(2,1)S(1)}, bf16[40,80,128]{2,1,0:T(8,128)(2,1)S(1)}, u32[]{:S(2)}, u32[]{:S(2)}) collective-permute-start(bf16[40,80,128]{2,1,0:T(8,128)(2,1)S(1)} %bitcast.26), channel_id=1, source_target_pairs={{0,1},{1,2},{2,3},{3,0},{4,5},{5,6},{6,7},{7,4},{8,9},{9,10},{10,1... | collective-permute-start | bytes 2457608 | tf_op jit(solution)/shard_map/ppermute | solution.py:38
  36.7 0.9 copy-start.5
  37.6 20.4 %collective-permute-start.1 = (bf16[40,80,128]{2,1,0:T(8,128)(2,1)S(1)}, bf16[40,80,128]{2,1,0:T(8,128)(2,1)}, u32[]{:S(2)}, u32[]{:S(2)}) collective-permute-start(bf16[40,80,128]{2,1,0:T(8,128)(2,1)S(1)} %collective-permute-done), channel_id=1, source_target_pairs={{0,1},{1,2},{2,3},{3,0},{4,5},{5,6},{6,7},{7,4},{8,9},{9,10},{10,1... | collective-permute-start | bytes 2457608 | tf_op jit(solution)/shard_map/ppermute | solution.py:38
  58.0 19.8 %collective-permute-start.2 = (bf16[40,80,128]{2,1,0:T(8,128)(2,1)}, bf16[40,80,128]{2,1,0:T(8,128)(2,1)}, u32[]{:S(2)}, u32[]{:S(2)}) collective-permute-start(bf16[40,80,128]{2,1,0:T(8,128)(2,1)} %collective-permute-done.1), channel_id=1, source_target_pairs={{0,1},{1,2},{2,3},{3,0},{4,5},{5,6},{6,7},{7,4},{8,9},{9,10},{10,1... | collective-permute-start | bytes 2457608 | tf_op jit(solution)/shard_map/ppermute | solution.py:38
  114.4 1.1 copy-start.4
  114.4 1.1 copy-start.11
  116.1 74.8 %copy-start.9 = (f32[128]{0:T(128)S(1)}, f32[128]{0:T(128)}, u32[]{:S(2)}) copy-start(f32[128]{0:T(128)} %param.14) | copy-start | bytes 1540
  116.1 74.8 %copy-start.10 = (f32[128]{0:T(128)S(1)}, f32[128]{0:T(128)}, u32[]{:S(2)}) copy-start(f32[128]{0:T(128)} %param.13) | copy-start | bytes 1540
  116.1 76.5 %copy-start.6 = (bf16[128,128]{1,0:T(8,128)(2,1)S(1)}, bf16[128,128]{1,0:T(8,128)(2,1)}, u32[]{:S(2)}) copy-start(bf16[128,128]{1,0:T(8,128)(2,1)} %param.15) | copy-start | bytes 98308
  186.7 4.2 %copy-start.2 = (bf16[40,80,128]{2,1,0:T(8,128)(2,1)S(1)}, bf16[40,80,128]{2,1,0:T(8,128)(2,1)}, u32[]{:S(2)}) copy-start(bf16[40,80,128]{2,1,0:T(8,128)(2,1)} %reduce-scatter.2.cloned.1.call-done) | copy-start | bytes 2457604
Sparse Core Ops, SparseCore 0:
  114.5 72.1 reduce-scatter.1
